TPU v7x, 512 devices: a whole 4x8x8 slice. The times are simulated.
512 devices in a mesh: tm: 64 (over z, y), state: 8 (over x, core).
Axes of the slice: x: 4, y: 8, z: 8, core: 2. Of those that a mesh axis runs over, the one named last changes fastest.
Arguments:
- offsets: int32 [5], replicated, may hold values from -3 to 3
- coefficients: float32 [5, 2048], replicated, may hold values from 0.1 to 1
- gain_matrix: bfloat16 [64, 1, 2048, 512], P('tm', None, 'state'), may hold values from -0.0625 to 0.0625
- direct_gain: float32 [64, 1, 512], P('tm'), may hold values from 0.2 to 0.8
- observed_cells: int32 [64, 1, 512], P('tm'), may hold values from 0 to 2047
- observed_values: float32 [64, 1, 512], P('tm'), may hold values from -4 to 4
Outputs:
- transition: float32 [64, 2048, 2048], P('tm', None, 'state')
- offset_term: float32 [64, 2048], P('tm')
All inputs are finite; a program needn't handle non-finite values.
Results may differ from a plain program's by a relative error of at most 0.0036.
Values may be sent and summed in bfloat16 or wider, within the bound.
A program may use at most 64 MiB of HBM per device.

v0:
```python
import jax
import jax.numpy as jnp
from jax import lax
from jax.sharding import PartitionSpec as P


def from_behind(value, axis, steps):
    count = lax.axis_size(axis)
    leading, last = (max(0, -steps), min(count, count - steps))
    return lax.ppermute(value, axis, [(source, source + steps) for source in range(leading, last)])


def advance(matrix, step_gains, cells_used, weights, offsets, forcing):
    spread = weights[0][:, None] * jnp.roll(matrix, -offsets[0], axis=0)
    for tap_index in range(1, weights.shape[0]):
        spread = spread + weights[tap_index][:, None] * jnp.roll(
            matrix, -offsets[tap_index], axis=0
        )
    picked = jnp.take(spread, cells_used[0], axis=0)
    if forcing is not None:
        picked = picked - forcing[0][:, None]
    correction = jnp.dot(
        step_gains[0], picked.astype(jnp.bfloat16), preferred_element_type=jnp.float32
    )
    matrix = spread - correction
    return matrix


def local_gain_rows(gain_matrix, direct_gain, observed_cells):
    row_count = gain_matrix.shape[2]
    first_row = lax.axis_index("state") * row_count
    cell_ids = first_row + lax.broadcasted_iota(jnp.int32, gain_matrix.shape[1:], 1)
    observed_hit = cell_ids == observed_cells[0][:, None, :]
    extra = jnp.where(
        observed_hit, direct_gain[0][:, None, :], jnp.zeros_like(direct_gain[0][:, None, :])
    )
    return (gain_matrix[0].astype(jnp.float32) + extra).astype(jnp.bfloat16)


def shards(offsets, coefficients, gain_matrix, direct_gain, observed_cells, observed_values):
    weights = coefficients / jnp.sum(coefficients, axis=0, keepdims=True)
    gain_rows = local_gain_rows(gain_matrix, direct_gain, observed_cells)
    gain_full = lax.all_gather(gain_rows, "state", axis=1, tiled=True)
    cells_used = observed_cells[0]
    forcing = observed_values[0]
    cell_count = gain_full.shape[1]
    columns = gain_rows.shape[1]
    first_column = lax.axis_index("state") * columns
    row_ids = lax.broadcasted_iota(jnp.int32, (cell_count, columns), 0)
    column_ids = first_column + lax.broadcasted_iota(jnp.int32, (cell_count, columns), 1)
    identity_panel = (row_ids == column_ids).astype(jnp.float32)
    span_index = lax.axis_index("tm")

    def own_map(matrix, forced_values=None):
        return advance(matrix, gain_full, cells_used, weights, offsets, forced_values)

    level_zero_trans = own_map(identity_panel)
    level_zero_shift = own_map(jnp.zeros((cell_count, 1), jnp.float32), forcing)
    left_trans, left_shift = from_behind((level_zero_trans, level_zero_shift), "tm", 1)
    level_one_trans = jnp.where(span_index >= 1, own_map(left_trans), level_zero_trans)
    level_one_shift = jnp.where(
        span_index >= 1, own_map(left_shift) + level_zero_shift, level_zero_shift
    )
    far_trans, far_shift = from_behind((level_one_trans, level_one_shift), "tm", 2)
    far_trans = jnp.where(span_index == 1, identity_panel, far_trans)
    earlier_gains, earlier_cells = from_behind((gain_full, cells_used), "tm", 1)
    carried_trans = own_map(
        advance(far_trans, earlier_gains, earlier_cells, weights, offsets, None)
    )
    carried_shift = own_map(
        advance(far_shift, earlier_gains, earlier_cells, weights, offsets, None)
    )
    first_carried = 1
    transition = jnp.where(span_index >= first_carried, carried_trans, level_one_trans)
    offset_term = jnp.where(span_index >= 2, carried_shift + level_one_shift, level_one_shift)
    return (transition[None], offset_term[:, 0][None])


def solution(mesh):
    in_specs = (
        P(),
        P(),
        P("tm", None, "state", None),
        P("tm", None, None),
        P("tm", None, None),
        P("tm", None, None),
    )
    out_specs = (P("tm", None, "state"), P("tm", None))
    return jax.shard_map(shards, mesh=mesh, in_specs=in_specs, out_specs=out_specs, check_vma=False)
```

profile of v0, /device:TPU:24, one launch (start us, length us, event | category | flops | bytes accessed | tf_op | source)
XLA Modules:
  0.0 283.7 jit_solution(14787118618400152176)
XLA Ops:
  7.2 0.0 all-gather.2.cloned.1.call-start
  7.2 1.8 fusion.67
  9.1 0.0 all-gather.2.cloned.1.call-update
  9.1 4.7 %collective-permute-start.3 = (s32[1,512]{1,0:T(1,128)}, s32[1,512]{1,0:T(1,128)S(1)}, u32[]{:S(2)}, u32[]{:S(2)}) collective-permute-start(s32[1,512]{1,0:T(1,128)} %bitcast.144), channel_id=1, source_target_pairs={{0,8},{8,16},{16,24},{24,32},{32,40},{40,48},{48,56},{56,64},{64,7... | collective-permute-start | bytes 6152 | tf_op jit(solution)/shard_map/ppermute | solution.py:10
  13.8 1.5 fusion.131
  18.6 0.9 reduce_sum.9
  19.5 0.7 compare_select_fusion.1
  20.2 0.9 broadcast_divide_fusion
  21.1 0.2 fusion.66
  21.3 5.6 %fusion.42 = f32[2048,256]{1,0:T(8,128)S(1)} fusion(s32[]{:T(128)S(6)} %select_n.189, f32[2048,256]{1,0:T(8,128)S(1)} %fusion.66, s32[]{:T(128)S(6)} %select_n.181, s32[]{:T(128)S(6)} %select_n.183, s32[]{:T(128)S(6)} %select_n.185, s32[]{:T(128)S(6)} %select_n.187, f32[2048]{0:T(1024)S(1)} %bitcast.127, f32[2048]{0:T(1024)S(1)} %bitcast.131, ...), kind=kLoop, calls=%fused_computation.88 | loop fusion | flops 7340032 | bytes 4235284 | tf_op jit(solution)/shard_map/add | solution.py:16
  27.0 0.0 copy-start.1
  27.0 0.0 copy-start.2
  27.0 1.6 gather_fusion
  28.6 0.4 fusion.89
  28.9 3.1 %gather_fusion.4 = f32[512]{0:T(512)S(1)} fusion(f32[2048]{0:T(1024)S(1)} %bitcast.119, s32[1024]{0:T(1024)S(1)} %pad_clamp_fusion.1), kind=kCustom, calls=%fused_computation.1.clone | custom fusion | bytes 6144 | tf_op jit(solution)/shard_map/jit(_take)/gather | solution.py:19
  32.1 0.0 copy-done.1
  32.1 0.0 copy-done.2
  32.1 12.9 %all-gather.2.cloned.1.call-done = bf16[1,2048,512]{2,1,0:T(8,128)(2,1)} async-done(((bf16[1,256,512]{2,1,0:T(8,128)(2,1)}), bf16[1,2048,512]{2,1,0:T(8,128)(2,1)}) %all-gather.2.cloned.1.call-update) | async-done | bytes 2097168 | tf_op jit(solution)/shard_map/all_gather | solution.py:43
  45.0 0.0 copy-start
  45.1 0.0 copy-start.3
  45.1 4.5 %convolution_subtract_fusion.3 = f32[2048,256]{1,0:T(8,128)} fusion(f32[2048,256]{1,0:T(8,128)} %copy-done.1, bf16[1,2048,512]{2,1,0:T(8,128)(2,1)} %all-gather.2.cloned.1.call-done, bf16[512,256]{1,0:T(8,128)(2,1)S(1)} %gather_fusion, pred[512]{0:T(512)(128)(4,1)S(1)} %get-tuple-element.9), kind=kOutput, calls=%fused_computation.43 | convolution fusion | flops 537526272 | bytes 6554112 | tf_op jit(solution)/shard_map/dot_general | solution.py:22
  49.6 4.6 %collective-permute-start = (f32[2048,256]{1,0:T(8,128)}, f32[2048,256]{1,0:T(8,128)}, u32[]{:S(2)}, u32[]{:S(2)}) collective-permute-start(f32[2048,256]{1,0:T(8,128)} %convolution_subtract_fusion.3), channel_id=1, source_target_pairs={{0,8},{8,16},{16,24},{24,32},{32,40},{40,48},{48,56},{56,64},{64,7... | collective-permute-start | bytes 6291464 | tf_op jit(solution)/shard_map/ppermute | solution.py:10
  54.2 0.0 copy-done
  54.2 0.0 copy-done.3
  54.2 0.6 fusion.11
  54.8 2.5 collective-permute-start.4
  57.3 0.0 collective-permute-done.3
  57.4 42.5 %collective-permute-done.4 = f32[2048,1]{0,1:T(1,128)S(1)} collective-permute-done((f32[2048,1]{0,1:T(1,128)S(1)}, f32[2048,1]{0,1:T(1,128)S(1)}, u32[]{:S(2)}, u32[]{:S(2)}) %collective-permute-start.4) | collective-permute-done | bytes 8224 | tf_op jit(solution)/shard_map/ppermute | solution.py:10
  99.9 0.2 fusion.92
  100.0 3.1 %gather_fusion.5 = f32[512]{0:T(512)S(1)} fusion(f32[2048]{0:T(1024)S(1)} %bitcast.122, s32[1024]{0:T(1024)S(1)} %pad_clamp_fusion.1), kind=kCustom, calls=%fused_computation.5.clone | custom fusion | bytes 6144 | tf_op jit(solution)/shard_map/jit(_take)/gather | solution.py:19
  103.2 0.6 fusion.10
  103.8 4.4 %collective-permute-start.5 = (f32[2048,1]{0,1:T(1,128)S(1)}, f32[2048,1]{0,1:T(1,128)S(1)}, u32[]{:S(2)}, u32[]{:S(2)}) collective-permute-start(f32[2048,1]{0,1:T(1,128)S(1)} %fusion.10), channel_id=1, source_target_pairs={{0,16},{8,24},{16,32},{24,40},{32,48},{40,56},{48,64},{56,72},{64,... | collective-permute-start | bytes 24584 | tf_op jit(solution)/shard_map/ppermute | solution.py:10
  108.3 3.1 %collective-permute-start.2 = (bf16[1,2048,512]{2,1,0:T(8,128)(2,1)S(1)}, bf16[1,2048,512]{2,1,0:T(8,128)(2,1)}, u32[]{:S(2)}, u32[]{:S(2)}) collective-permute-start(bf16[1,2048,512]{2,1,0:T(8,128)(2,1)S(1)} %copy-done), channel_id=1, source_target_pairs={{0,8},{8,16},{16,24},{24,32},{32,40},{40,48},{48,56},{56,64},{64,7... | collective-permute-start | bytes 6291464 | tf_op jit(solution)/shard_map/ppermute | solution.py:10
  111.4 0.0 collective-permute-done.5
  111.4 0.0 collective-permute-done
  111.4 1.7 constant_dynamic-update-slice_fusion.1
  113.2 1.7 constant_dynamic-update-slice_fusion
  114.9 3.1 %fusion.62 = f32[2048,256]{1,0:T(8,128)} fusion(f32[4096,256]{1,0:T(8,128)S(1)} %constant_dynamic-update-slice_fusion, s32[]{:T(128)S(6)} %select_n.189, s32[]{:T(128)S(6)} %select_n.187, s32[]{:T(128)S(6)} %select_n.185, s32[]{:T(128)S(6)} %select_n.183, s32[]{:T(128)S(6)} %select_n.181, f32[2048]{0:T(1024)S(1)} %bitcast.128, f32[2048]{0:T(1024)S(1)} %bitcast.132, ...), kind=kLoop, calls=%fused_computation.109 | loop fusion | flops 4718592 | bytes 12623892 | tf_op jit(solution)/shard_map/add | solution.py:16
  118.0 3.1 %gather_fusion.1 = bf16[512,256]{1,0:T(8,128)(2,1)S(1)} fusion(f32[2048,256]{1,0:T(8,128)} %fusion.62, s32[1024]{0:T(1024)S(1)} %pad_clamp_fusion.1), kind=kCustom, calls=%fused_computation.2.clone | custom fusion | bytes 526336 | tf_op jit(solution)/shard_map/jit(_take)/gather | solution.py:19
  121.1 3.7 %fusion.1 = f32[2048,256]{1,0:T(8,128)} fusion(f32[2048,256]{1,0:T(8,128)} %convolution_subtract_fusion.3, f32[2048,256]{1,0:T(8,128)} %fusion.62, bf16[1,2048,512]{2,1,0:T(8,128)(2,1)S(1)} %copy-done, pred[]{:T(512)S(6)} %ge.18, bf16[512,256]{1,0:T(8,128)(2,1)S(1)} %gather_fusion.1, pred[512]{0:T(512)(128)(4,1)S(1)} %get-tuple-element.9), kind=kOutput, calls=%fused_computation.42 | convolution fusion | flops 538050560 | bytes 8651265 | tf_op jit(solution)/shard_map/dot_general | solution.py:22
  124.9 5.1 %collective-permute-start.1 = (f32[2048,256]{1,0:T(8,128)}, f32[2048,256]{1,0:T(8,128)}, u32[]{:S(2)}, u32[]{:S(2)}) collective-permute-start(f32[2048,256]{1,0:T(8,128)} %fusion.1), channel_id=1, source_target_pairs={{0,16},{8,24},{16,32},{24,40},{32,48},{40,56},{48,64},{56,72},{64,... | collective-permute-start | bytes 6291464 | tf_op jit(solution)/shard_map/ppermute | solution.py:10
  130.0 0.2 fusion.94
  130.1 3.1 %gather_fusion.6 = f32[512]{0:T(512)S(1)} fusion(f32[2048]{0:T(1024)S(1)} %bitcast.120, s32[1024]{0:T(1024)S(1)} %pad_clamp_fusion), kind=kCustom, calls=%fused_computation.6.clone | custom fusion | bytes 6144 | tf_op jit(solution)/shard_map/jit(_take)/gather | solution.py:19
  133.3 26.4 %collective-permute-done.2 = bf16[1,2048,512]{2,1,0:T(8,128)(2,1)} collective-permute-done((bf16[1,2048,512]{2,1,0:T(8,128)(2,1)S(1)}, bf16[1,2048,512]{2,1,0:T(8,128)(2,1)}, u32[]{:S(2)}, u32[]{:S(2)}) %collective-permute-start.2) | collective-permute-done | bytes 2097184 | tf_op jit(solution)/shard_map/ppermute | solution.py:10
  159.7 2.2 fusion.7
  161.9 0.4 fusion.97
  162.3 3.1 %gather_fusion.7 = f32[512]{0:T(512)S(1)} fusion(f32[2048]{0:T(1024)S(1)} %bitcast.121, s32[1024]{0:T(1024)S(1)} %pad_clamp_fusion.1), kind=kCustom, calls=%fused_computation.7.clone | custom fusion | bytes 6144 | tf_op jit(solution)/shard_map/jit(_take)/gather | solution.py:19
  165.5 1.3 fusion.6
  166.7 82.3 %collective-permute-done.1 = f32[2048,256]{1,0:T(8,128)} collective-permute-done((f32[2048,256]{1,0:T(8,128)}, f32[2048,256]{1,0:T(8,128)}, u32[]{:S(2)}, u32[]{:S(2)}) %collective-permute-start.1) | collective-permute-done | bytes 2097184 | tf_op jit(solution)/shard_map/ppermute | solution.py:10
  249.0 1.9 broadcast_select_fusion
  250.9 6.4 %fusion.28 = f32[2048,256]{1,0:T(8,128)} fusion(s32[]{:T(128)S(6)} %select_n.189, f32[2048,256]{1,0:T(8,128)S(1)} %broadcast_select_fusion, s32[]{:T(128)S(6)} %select_n.181, s32[]{:T(128)S(6)} %select_n.183, s32[]{:T(128)S(6)} %select_n.185, s32[]{:T(128)S(6)} %select_n.187, f32[2048]{0:T(1024)S(1)} %bitcast.129, f32[2048]{0:T(1024)S(1)} %bitcast.133, ...), kind=kLoop, calls=%fused_computation.74 | loop fusion | flops 7340032 | bytes 4235284 | tf_op jit(solution)/shard_map/add | solution.py:16
  257.3 3.1 %gather_fusion.2 = bf16[512,256]{1,0:T(8,128)(2,1)S(1)} fusion(f32[2048,256]{1,0:T(8,128)} %fusion.28, s32[1024]{0:T(1024)S(1)} %pad_clamp_fusion), kind=kCustom, calls=%fused_computation.3.clone | custom fusion | bytes 526336 | tf_op jit(solution)/shard_map/jit(_take)/gather | solution.py:19
  260.5 3.0 %convolution_subtract_fusion.1 = f32[2048,256]{1,0:T(8,128)S(1)} fusion(f32[2048,256]{1,0:T(8,128)} %fusion.28, bf16[1,2048,512]{2,1,0:T(8,128)(2,1)} %collective-permute-done.2, bf16[512,256]{1,0:T(8,128)(2,1)S(1)} %gather_fusion.2, pred[512]{0:T(512)(128)(4,1)S(1)} %get-tuple-element.6), kind=kOutput, calls=%fused_computation.40 | convolution fusion | flops 537526272 | bytes 6554112 | tf_op jit(solution)/shard_map/dot_general | solution.py:22
  263.5 6.4 %fusion.14 = f32[2048,256]{1,0:T(8,128)} fusion(s32[]{:T(128)S(6)} %select_n.189, f32[2048,256]{1,0:T(8,128)S(1)} %convolution_subtract_fusion.1, s32[]{:T(128)S(6)} %select_n.181, s32[]{:T(128)S(6)} %select_n.183, s32[]{:T(128)S(6)} %select_n.185, s32[]{:T(128)S(6)} %select_n.187, f32[2048]{0:T(1024)S(1)} %bitcast.130, f32[2048]{0:T(1024)S(1)} %bitcast.134, ...), kind=kLoop, calls=%fused_computation.60 | loop fusion | flops 7340032 | bytes 4235284 | tf_op jit(solution)/shard_map/add | solution.py:16
  270.0 3.1 %gather_fusion.3 = bf16[512,256]{1,0:T(8,128)(2,1)S(1)} fusion(f32[2048,256]{1,0:T(8,128)} %fusion.14, s32[1024]{0:T(1024)S(1)} %pad_clamp_fusion.1), kind=kCustom, calls=%fused_computation.4.clone | custom fusion | bytes 526336 | tf_op jit(solution)/shard_map/jit(_take)/gather | solution.py:19
  273.1 3.7 %fusion.2 = f32[1,2048,256]{2,1,0:T(8,128)} fusion(f32[2048,256]{1,0:T(8,128)} %fusion.1, f32[2048,256]{1,0:T(8,128)} %fusion.14, bf16[1,2048,512]{2,1,0:T(8,128)(2,1)S(1)} %copy-done, pred[]{:T(512)S(6)} %ge.18, bf16[512,256]{1,0:T(8,128)(2,1)S(1)} %gather_fusion.3, pred[512]{0:T(512)(128)(4,1)S(1)} %get-tuple-element.9), kind=kOutput, calls=%fused_computation.44 | convolution fusion | flops 538050560 | bytes 8651265 | tf_op jit(solution)/shard_map/dot_general | solution.py:22
  (14 shorter events, 0.1 us)
Async XLA Ops:
  7.2 37.9 %all-gather.2.cloned.1.call-start = ((), (), s32[]{:S(2)}) async-start(), calls=%async_computation | async-start | bytes 2359296 | tf_op jit(solution)/shard_map/all_gather | solution.py:43
  9.1 48.3 %collective-permute-start.3 = (s32[1,512]{1,0:T(1,128)}, s32[1,512]{1,0:T(1,128)S(1)}, u32[]{:S(2)}, u32[]{:S(2)}) collective-permute-start(s32[1,512]{1,0:T(1,128)} %bitcast.144), channel_id=1, source_target_pairs={{0,8},{8,16},{16,24},{24,32},{32,40},{40,48},{48,56},{56,64},{64,7... | collective-permute-start | bytes 6152 | tf_op jit(solution)/shard_map/ppermute | solution.py:10
  27.0 5.1 %copy-start.1 = (f32[2048,256]{1,0:T(8,128)}, f32[2048,256]{1,0:T(8,128)S(1)}, u32[]{:S(2)}) copy-start(f32[2048,256]{1,0:T(8,128)S(1)} %fusion.42) | copy-start | bytes 6291460
  27.0 5.1 %copy-start.2 = (s32[1,1,512]{2,1,0:T(1,128)S(1)}, s32[1,1,512]{2,1,0:T(1,128)}, u32[]{:S(2)}) copy-start(s32[1,1,512]{2,1,0:T(1,128)} %param.18) | copy-start | bytes 6148
  45.0 9.1 %copy-start = (bf16[1,2048,512]{2,1,0:T(8,128)(2,1)S(1)}, bf16[1,2048,512]{2,1,0:T(8,128)(2,1)}, u32[]{:S(2)}) copy-start(bf16[1,2048,512]{2,1,0:T(8,128)(2,1)} %all-gather.2.cloned.1.call-done) | copy-start | bytes 6291460
  45.1 9.1 %copy-start.3 = (f32[1,1,512]{2,1,0:T(1,128)S(1)}, f32[1,1,512]{2,1,0:T(1,128)}, u32[]{:S(2)}) copy-start(f32[1,1,512]{2,1,0:T(1,128)} %param.19) | copy-start | bytes 6148
  49.6 61.9 %collective-permute-start = (f32[2048,256]{1,0:T(8,128)}, f32[2048,256]{1,0:T(8,128)}, u32[]{:S(2)}, u32[]{:S(2)}) collective-permute-start(f32[2048,256]{1,0:T(8,128)} %convolution_subtract_fusion.3), channel_id=1, source_target_pairs={{0,8},{8,16},{16,24},{24,32},{32,40},{40,48},{48,56},{56,64},{64,7... | collective-permute-start | bytes 6291464 | tf_op jit(solution)/shard_map/ppermute | solution.py:10
  54.8 45.0 %collective-permute-start.4 = (f32[2048,1]{0,1:T(1,128)S(1)}, f32[2048,1]{0,1:T(1,128)S(1)}, u32[]{:S(2)}, u32[]{:S(2)}) collective-permute-start(f32[2048,1]{0,1:T(1,128)S(1)} %fusion.11), channel_id=1, source_target_pairs={{0,8},{8,16},{16,24},{24,32},{32,40},{40,48},{48,56},{56,64},{64,7... | collective-permute-start | bytes 24584 | tf_op jit(solution)/shard_map/ppermute | solution.py:10
  103.8 7.6 %collective-permute-start.5 = (f32[2048,1]{0,1:T(1,128)S(1)}, f32[2048,1]{0,1:T(1,128)S(1)}, u32[]{:S(2)}, u32[]{:S(2)}) collective-permute-start(f32[2048,1]{0,1:T(1,128)S(1)} %fusion.10), channel_id=1, source_target_pairs={{0,16},{8,24},{16,32},{24,40},{32,48},{40,56},{48,64},{56,72},{64,... | collective-permute-start | bytes 24584 | tf_op jit(solution)/shard_map/ppermute | solution.py:10
  108.3 51.4 %collective-permute-start.2 = (bf16[1,2048,512]{2,1,0:T(8,128)(2,1)S(1)}, bf16[1,2048,512]{2,1,0:T(8,128)(2,1)}, u32[]{:S(2)}, u32[]{:S(2)}) collective-permute-start(bf16[1,2048,512]{2,1,0:T(8,128)(2,1)S(1)} %copy-done), channel_id=1, source_target_pairs={{0,8},{8,16},{16,24},{24,32},{32,40},{40,48},{48,56},{56,64},{64,7... | collective-permute-start | bytes 6291464 | tf_op jit(solution)/shard_map/ppermute | solution.py:10
  124.9 124.1 %collective-permute-start.1 = (f32[2048,256]{1,0:T(8,128)}, f32[2048,256]{1,0:T(8,128)}, u32[]{:S(2)}, u32[]{:S(2)}) collective-permute-start(f32[2048,256]{1,0:T(8,128)} %fusion.1), channel_id=1, source_target_pairs={{0,16},{8,24},{16,32},{24,40},{32,48},{40,56},{48,64},{56,72},{64,... | collective-permute-start | bytes 6291464 | tf_op jit(solution)/shard_map/ppermute | solution.py:10
Sparse Core Ops, SparseCore 0:
  10.1 34.8 all-gather.1
where the time goes:
time: 284 us
  waiting for transfers between devices  164 us (58%)
  other arithmetic  29.1 us (10%)
  local copies, waits for them, and re-layouts  28.6 us (10%)
  starting transfers between devices  24.4 us (9%)
  matrix products  19.8 us (7%)
  between operations  17.7 us (6%)
    ppermute x6, waiting for transfers between devices, from_behind(): lax.ppermute(value, axis, [(source, source + steps) for source in range(l...  151 us
    ppermute x6, starting transfers between devices, from_behind(): lax.ppermute(value, axis, [(source, source + steps) for source in range(l...  24.4 us
    gather x8, local copies, waits for them, and re-layouts, advance(): picked = jnp.take(spread, cells_used[0], axis=0)  23.6 us
    add x8, other arithmetic, advance(): spread + weights[tap_index][:, None] * jnp.roll(matrix, -offsets[tap_inde...  22.7 us
    dot_general x8, matrix products, advance(): jnp.dot(step_gains[0], picked.astype(jnp.bfloat16), preferred_element_typ...  19.8 us
    all_gather x1, waiting for transfers between devices, shards(): gain_full = lax.all_gather(gain_rows, 'state', axis=1, tiled=True)  12.9 us
  transfers between devices with their start and end apart: 7, of which 4 were waited for; matrix products, arithmetic and copies ran while one was open for 17% of the time, Pallas kernels for 0%

commit v1 on v0

--- a/solution.py
+++ b/solution.py
@@ -2,6 +2,12 @@
 import jax.numpy as jnp
 from jax import lax
 from jax.sharding import PartitionSpec as P
+
+
+def tiled_gather(x, axis, dim):
+    size = lax.axis_size(axis)
+    repeats = [size if d == dim else 1 for d in range(x.ndim)]
+    return lax.all_to_all(jnp.tile(x, repeats), axis, split_axis=dim, concat_axis=dim, tiled=True)
 
 
 def from_behind(value, axis, steps):
@@ -40,7 +46,7 @@
 def shards(offsets, coefficients, gain_matrix, direct_gain, observed_cells, observed_values):
     weights = coefficients / jnp.sum(coefficients, axis=0, keepdims=True)
     gain_rows = local_gain_rows(gain_matrix, direct_gain, observed_cells)
-    gain_full = lax.all_gather(gain_rows, "state", axis=1, tiled=True)
+    gain_full = tiled_gather(gain_rows, "state", 1)
     cells_used = observed_cells[0]
     forcing = observed_values[0]
     cell_count = gain_full.shape[1]

time: 284 us -> 312 us (1.099)
  the two profiles are of different devices: /device:TPU:24 before, /device:TPU:248 now
where the time goes in v1:
time: 312 us; the launch traced here: 311 us
  waiting for transfers between devices  155 us (50%)
  local copies, waits for them, and re-layouts  60.5 us (19%)
  other arithmetic  40.1 us (13%)
  starting transfers between devices  33.3 us (11%)
  matrix products  17.4 us (6%)
  between operations  4.23 us (1%)
    ppermute x6, waiting for transfers between devices, from_behind(): lax.ppermute(value, axis, [(source, source + steps) for source in range(l...  148 us
    ppermute x6, starting transfers between devices, from_behind(): lax.ppermute(value, axis, [(source, source + steps) for source in range(l...  28.9 us
    gather x8, local copies, waits for them, and re-layouts, advance(): picked = jnp.take(spread, cells_used[0], axis=0)  23.6 us
    add x8, other arithmetic, advance(): spread + weights[tap_index][:, None] * jnp.roll(matrix, -offsets[tap_inde...  22.7 us
    another operation x2, local copies, waits for them, and re-layouts, tiled_gather(): jnp.tile(x, repeats)  18.7 us
    dot_general x8, matrix products, advance(): jnp.dot(step_gains[0], picked.astype(jnp.bfloat16), preferred_element_typ...  17.4 us
    unnamed x19, local copies, waits for them, and re-layouts  15.8 us
    unnamed x1, other arithmetic  14.1 us
  transfers between devices with their start and end apart: 7, of which 4 were waited for; matrix products, arithmetic and copies ran while one was open for 17% of the time, Pallas kernels for 0%

profile of v1, /device:TPU:248, one launch (start us, length us, event | category | flops | bytes accessed | tf_op | source)
XLA Modules:
  0.0 310.7 jit_solution(15900010952574923027)
XLA Ops:
  0.6 1.1 fusion.67
  1.8 0.2 tile.4
  1.9 18.5 %copy.12 = bf16[1,2048,512]{2,0,1:T(2,128)(2,1)} copy(bf16[1,2048,512]{2,1,0:T(8,128)(2,1)S(1)} %bitcast.130) | data formatting | bytes 4194304 | tf_op jit(solution)/shard_map/tile | solution.py:10
  20.5 0.5 broadcast.97
  21.0 14.1 %reduce = bf16[2048,512]{1,0:T(8,128)(2,1)S(1)} reduce(bf16[2048,1,512]{2,1,0:T(2,128)(2,1)} %bitcast.128, bf16[]{:T(256)} %broadcast.97), dimensions={1}, to_apply=%bitcast.123.reduce_sub_computation | reduce | bytes 4194306
  35.1 3.8 %reshape.247 = bf16[8,2,65536]{2,1,0:T(2,128)(2,1)} reshape(bf16[2048,512]{1,0:T(8,128)(2,1)S(1)} %reduce) | data formatting | bytes 4194304
  38.9 0.0 copy-start.3
  38.9 0.0 copy-start.2
  38.9 0.0 copy-start.4
  38.9 4.5 %all-to-all-start = ((bf16[8,2,65536]{2,1,0:T(2,128)(2,1)}), bf16[8,2,65536]{2,1,0:T(2,128)(2,1)}, u32[]{:S(2)}, u32[]{:S(2)}) async-start(bf16[8,2,65536]{2,1,0:T(2,128)(2,1)} %reshape.247), calls=%async_computation | async-start | bytes 4194304 | tf_op jit(solution)/shard_map/all_to_all | solution.py:10
  43.4 0.0 copy-done.3
  43.4 4.7 %collective-permute-start.3 = (s32[1,512]{1,0:T(1,128)S(1)}, s32[1,512]{1,0:T(1,128)S(1)}, u32[]{:S(2)}, u32[]{:S(2)}) collective-permute-start(s32[1,512]{1,0:T(1,128)S(1)} %bitcast.152), channel_id=1, source_target_pairs={{0,8},{8,16},{16,24},{24,32},{32,40},{40,48},{48,56},{56,64},{64,7... | collective-permute-start | bytes 6152 | tf_op jit(solution)/shard_map/ppermute | solution.py:16
  48.1 0.0 copy-done.2
  48.2 0.0 copy-done.4
  48.2 0.6 fusion.131
  52.1 0.2 fusion.66
  52.3 5.6 %fusion.42 = f32[2048,256]{1,0:T(8,128)S(1)} fusion(s32[]{:T(128)S(6)} %select_n.187, f32[2048,256]{1,0:T(8,128)S(1)} %fusion.66, s32[]{:T(128)S(6)} %select_n.179, s32[]{:T(128)S(6)} %select_n.181, s32[]{:T(128)S(6)} %select_n.183, s32[]{:T(128)S(6)} %select_n.185, f32[2048]{0:T(1024)S(1)} %bitcast.135, f32[2048]{0:T(1024)S(1)} %bitcast.139, ...), kind=kLoop, calls=%fused_computation.88 | loop fusion | flops 7340032 | bytes 4235284 | tf_op jit(solution)/shard_map/add | solution.py:22
  57.9 0.0 copy-start
  57.9 1.6 gather_fusion
  59.5 0.4 fusion.89
  59.9 3.1 %gather_fusion.4 = f32[512]{0:T(512)S(1)} fusion(f32[2048]{0:T(1024)S(1)} %bitcast.124, s32[1024]{0:T(1024)S(1)} %pad_clamp_fusion.1), kind=kCustom, calls=%fused_computation.1.clone | custom fusion | bytes 6144 | tf_op jit(solution)/shard_map/jit(_take)/gather | solution.py:25
  63.0 0.0 copy-done
  63.1 7.6 %all-to-all-done = bf16[8,2,65536]{2,1,0:T(2,128)(2,1)} async-done(((bf16[8,2,65536]{2,1,0:T(2,128)(2,1)}), bf16[8,2,65536]{2,1,0:T(2,128)(2,1)}, u32[]{:S(2)}, u32[]{:S(2)}) %all-to-all-start) | async-done | bytes 2097184 | tf_op jit(solution)/shard_map/all_to_all | solution.py:10
  70.6 6.8 %reshape.248 = bf16[2048,1,512]{2,1,0:T(2,128)(2,1)} reshape(bf16[8,2,65536]{2,1,0:T(2,128)(2,1)} %all-to-all-done) | data formatting | bytes 4194304
  77.4 0.0 copy-start.1
  77.4 2.9 copy.10
  80.3 0.0 copy-done.1
  80.3 0.0 copy-start.5
  80.4 2.1 convolution_subtract_fusion.3
  82.5 4.7 %collective-permute-start = (f32[2048,256]{1,0:T(8,128)}, f32[2048,256]{1,0:T(8,128)}, u32[]{:S(2)}, u32[]{:S(2)}) collective-permute-start(f32[2048,256]{1,0:T(8,128)} %convolution_subtract_fusion.3), channel_id=1, source_target_pairs={{0,8},{8,16},{16,24},{24,32},{32,40},{40,48},{48,56},{56,64},{64,7... | collective-permute-start | bytes 6291464 | tf_op jit(solution)/shard_map/ppermute | solution.py:16
  87.2 0.0 copy-done.5
  87.2 0.6 fusion.11
  87.8 3.5 %collective-permute-start.4 = (f32[2048,1]{0,1:T(1,128)S(1)}, f32[2048,1]{0,1:T(1,128)S(1)}, u32[]{:S(2)}, u32[]{:S(2)}) collective-permute-start(f32[2048,1]{0,1:T(1,128)S(1)} %fusion.11), channel_id=1, source_target_pairs={{0,8},{8,16},{16,24},{24,32},{32,40},{40,48},{48,56},{56,64},{64,7... | collective-permute-start | bytes 24584 | tf_op jit(solution)/shard_map/ppermute | solution.py:16
  91.3 0.0 collective-permute-done.3
  91.4 40.9 %collective-permute-done.4 = f32[2048,1]{0,1:T(1,128)S(1)} collective-permute-done((f32[2048,1]{0,1:T(1,128)S(1)}, f32[2048,1]{0,1:T(1,128)S(1)}, u32[]{:S(2)}, u32[]{:S(2)}) %collective-permute-start.4) | collective-permute-done | bytes 8224 | tf_op jit(solution)/shard_map/ppermute | solution.py:16
  132.3 0.2 fusion.92
  132.4 3.1 %gather_fusion.5 = f32[512]{0:T(512)S(1)} fusion(f32[2048]{0:T(1024)S(1)} %bitcast.127, s32[1024]{0:T(1024)S(1)} %pad_clamp_fusion.1), kind=kCustom, calls=%fused_computation.5.clone | custom fusion | bytes 6144 | tf_op jit(solution)/shard_map/jit(_take)/gather | solution.py:25
  135.6 0.6 fusion.10
  136.2 5.4 %collective-permute-start.5 = (f32[2048,1]{0,1:T(1,128)S(1)}, f32[2048,1]{0,1:T(1,128)S(1)}, u32[]{:S(2)}, u32[]{:S(2)}) collective-permute-start(f32[2048,1]{0,1:T(1,128)S(1)} %fusion.10), channel_id=1, source_target_pairs={{0,16},{8,24},{16,32},{24,40},{32,48},{40,56},{48,64},{56,72},{64,... | collective-permute-start | bytes 24584 | tf_op jit(solution)/shard_map/ppermute | solution.py:16
  141.7 4.4 %collective-permute-start.2 = (bf16[1,2048,512]{2,1,0:T(8,128)(2,1)S(1)}, bf16[1,2048,512]{2,1,0:T(8,128)(2,1)}, u32[]{:S(2)}, u32[]{:S(2)}) collective-permute-start(bf16[1,2048,512]{2,1,0:T(8,128)(2,1)S(1)} %copy.10), channel_id=1, source_target_pairs={{0,8},{8,16},{16,24},{24,32},{32,40},{40,48},{48,56},{56,64},{64,7... | collective-permute-start | bytes 6291464 | tf_op jit(solution)/shard_map/ppermute | solution.py:16
  146.1 0.0 collective-permute-done.5
  146.1 0.0 collective-permute-done
  146.1 1.7 constant_dynamic-update-slice_fusion.1
  147.9 1.7 constant_dynamic-update-slice_fusion
  149.6 3.1 %fusion.62 = f32[2048,256]{1,0:T(8,128)} fusion(f32[4096,256]{1,0:T(8,128)S(1)} %constant_dynamic-update-slice_fusion, s32[]{:T(128)S(6)} %select_n.187, s32[]{:T(128)S(6)} %select_n.185, s32[]{:T(128)S(6)} %select_n.183, s32[]{:T(128)S(6)} %select_n.181, s32[]{:T(128)S(6)} %select_n.179, f32[2048]{0:T(1024)S(1)} %bitcast.136, f32[2048]{0:T(1024)S(1)} %bitcast.140, ...), kind=kLoop, calls=%fused_computation.109 | loop fusion | flops 4718592 | bytes 12623892 | tf_op jit(solution)/shard_map/add | solution.py:22
  152.7 3.1 %gather_fusion.1 = bf16[512,256]{1,0:T(8,128)(2,1)S(1)} fusion(f32[2048,256]{1,0:T(8,128)} %fusion.62, s32[1024]{0:T(1024)S(1)} %pad_clamp_fusion.1), kind=kCustom, calls=%fused_computation.2.clone | custom fusion | bytes 526336 | tf_op jit(solution)/shard_map/jit(_take)/gather | solution.py:25
  155.9 3.7 %fusion.1 = f32[2048,256]{1,0:T(8,128)} fusion(f32[2048,256]{1,0:T(8,128)} %convolution_subtract_fusion.3, f32[2048,256]{1,0:T(8,128)} %fusion.62, bf16[1,2048,512]{2,1,0:T(8,128)(2,1)S(1)} %copy.10, pred[]{:T(512)S(6)} %ge.18, bf16[512,256]{1,0:T(8,128)(2,1)S(1)} %gather_fusion.1, pred[512]{0:T(512)(128)(4,1)S(1)} %get-tuple-element.9), kind=kOutput, calls=%fused_computation.42 | convolution fusion | flops 538050560 | bytes 8651265 | tf_op jit(solution)/shard_map/dot_general | solution.py:28
  159.6 6.2 %collective-permute-start.1 = (f32[2048,256]{1,0:T(8,128)}, f32[2048,256]{1,0:T(8,128)}, u32[]{:S(2)}, u32[]{:S(2)}) collective-permute-start(f32[2048,256]{1,0:T(8,128)} %fusion.1), channel_id=1, source_target_pairs={{0,16},{8,24},{16,32},{24,40},{32,48},{40,56},{48,64},{56,72},{64,... | collective-permute-start | bytes 6291464 | tf_op jit(solution)/shard_map/ppermute | solution.py:16
  165.8 0.2 fusion.94
  166.0 3.1 %gather_fusion.6 = f32[512]{0:T(512)S(1)} fusion(f32[2048]{0:T(1024)S(1)} %bitcast.125, s32[1024]{0:T(1024)S(1)} %pad_clamp_fusion), kind=kCustom, calls=%fused_computation.6.clone | custom fusion | bytes 6144 | tf_op jit(solution)/shard_map/jit(_take)/gather | solution.py:25
  169.1 67.1 %collective-permute-done.2 = bf16[1,2048,512]{2,1,0:T(8,128)(2,1)} collective-permute-done((bf16[1,2048,512]{2,1,0:T(8,128)(2,1)S(1)}, bf16[1,2048,512]{2,1,0:T(8,128)(2,1)}, u32[]{:S(2)}, u32[]{:S(2)}) %collective-permute-start.2) | collective-permute-done | bytes 2097184 | tf_op jit(solution)/shard_map/ppermute | solution.py:16
  236.2 2.2 fusion.7
  238.4 0.4 fusion.97
  238.8 3.1 %gather_fusion.7 = f32[512]{0:T(512)S(1)} fusion(f32[2048]{0:T(1024)S(1)} %bitcast.126, s32[1024]{0:T(1024)S(1)} %pad_clamp_fusion.1), kind=kCustom, calls=%fused_computation.7.clone | custom fusion | bytes 6144 | tf_op jit(solution)/shard_map/jit(_take)/gather | solution.py:25
  242.0 1.3 fusion.6
  243.2 39.6 %collective-permute-done.1 = f32[2048,256]{1,0:T(8,128)} collective-permute-done((f32[2048,256]{1,0:T(8,128)}, f32[2048,256]{1,0:T(8,128)}, u32[]{:S(2)}, u32[]{:S(2)}) %collective-permute-start.1) | collective-permute-done | bytes 2097184 | tf_op jit(solution)/shard_map/ppermute | solution.py:16
  282.8 1.9 broadcast_select_fusion
  284.7 6.4 %fusion.28 = f32[2048,256]{1,0:T(8,128)} fusion(s32[]{:T(128)S(6)} %select_n.187, f32[2048,256]{1,0:T(8,128)S(1)} %broadcast_select_fusion, s32[]{:T(128)S(6)} %select_n.179, s32[]{:T(128)S(6)} %select_n.181, s32[]{:T(128)S(6)} %select_n.183, s32[]{:T(128)S(6)} %select_n.185, f32[2048]{0:T(1024)S(1)} %bitcast.137, f32[2048]{0:T(1024)S(1)} %bitcast.141, ...), kind=kLoop, calls=%fused_computation.74 | loop fusion | flops 7340032 | bytes 4235284 | tf_op jit(solution)/shard_map/add | solution.py:22
  291.1 3.1 %gather_fusion.2 = bf16[512,256]{1,0:T(8,128)(2,1)S(1)} fusion(f32[2048,256]{1,0:T(8,128)} %fusion.28, s32[1024]{0:T(1024)S(1)} %pad_clamp_fusion), kind=kCustom, calls=%fused_computation.3.clone | custom fusion | bytes 526336 | tf_op jit(solution)/shard_map/jit(_take)/gather | solution.py:25
  294.3 3.0 convolution_subtract_fusion.1
  297.3 6.4 %fusion.14 = f32[2048,256]{1,0:T(8,128)} fusion(s32[]{:T(128)S(6)} %select_n.187, f32[2048,256]{1,0:T(8,128)S(1)} %convolution_subtract_fusion.1, s32[]{:T(128)S(6)} %select_n.179, s32[]{:T(128)S(6)} %select_n.181, s32[]{:T(128)S(6)} %select_n.183, s32[]{:T(128)S(6)} %select_n.185, f32[2048]{0:T(1024)S(1)} %bitcast.138, f32[2048]{0:T(1024)S(1)} %bitcast.142, ...), kind=kLoop, calls=%fused_computation.60 | loop fusion | flops 7340032 | bytes 4235284 | tf_op jit(solution)/shard_map/add | solution.py:22
  303.8 3.1 %gather_fusion.3 = bf16[512,256]{1,0:T(8,128)(2,1)S(1)} fusion(f32[2048,256]{1,0:T(8,128)} %fusion.14, s32[1024]{0:T(1024)S(1)} %pad_clamp_fusion.1), kind=kCustom, calls=%fused_computation.4.clone | custom fusion | bytes 526336 | tf_op jit(solution)/shard_map/jit(_take)/gather | solution.py:25
  306.9 3.7 %fusion.2 = f32[1,2048,256]{2,1,0:T(8,128)} fusion(f32[2048,256]{1,0:T(8,128)} %fusion.1, f32[2048,256]{1,0:T(8,128)} %fusion.14, bf16[1,2048,512]{2,1,0:T(8,128)(2,1)S(1)} %copy.10, pred[]{:T(512)S(6)} %ge.18, bf16[512,256]{1,0:T(8,128)(2,1)S(1)} %gather_fusion.3, pred[512]{0:T(512)(128)(4,1)S(1)} %get-tuple-element.9), kind=kOutput, calls=%fused_computation.44 | convolution fusion | flops 538050560 | bytes 8651265 | tf_op jit(solution)/shard_map/dot_general | solution.py:28
  (17 shorter events, 0.2 us)
Async XLA Ops:
  38.9 4.5 %copy-start.3 = (s32[1,1,512]{2,1,0:T(1,128)S(1)}, s32[1,1,512]{2,1,0:T(1,128)}, u32[]{:S(2)}) copy-start(s32[1,1,512]{2,1,0:T(1,128)} %param.18) | copy-start | bytes 6148
  38.9 9.2 %copy-start.2 = (f32[5,2048]{1,0:T(8,128)S(1)}, f32[5,2048]{1,0:T(8,128)}, u32[]{:S(2)}) copy-start(f32[5,2048]{1,0:T(8,128)} %param.15) | copy-start | bytes 122884
  38.9 9.3 %copy-start.4 = (s32[5]{0:T(128)S(1)}, s32[5]{0:T(128)}, u32[]{:S(2)}) copy-start(s32[5]{0:T(128)} %param.14) | copy-start | bytes 64
  38.9 31.7 %all-to-all-start = ((bf16[8,2,65536]{2,1,0:T(2,128)(2,1)}), bf16[8,2,65536]{2,1,0:T(2,128)(2,1)}, u32[]{:S(2)}, u32[]{:S(2)}) async-start(bf16[8,2,65536]{2,1,0:T(2,128)(2,1)} %reshape.247), calls=%async_computation | async-start | bytes 4194304 | tf_op jit(solution)/shard_map/all_to_all | solution.py:10
  43.4 47.9 %collective-permute-start.3 = (s32[1,512]{1,0:T(1,128)S(1)}, s32[1,512]{1,0:T(1,128)S(1)}, u32[]{:S(2)}, u32[]{:S(2)}) collective-permute-start(s32[1,512]{1,0:T(1,128)S(1)} %bitcast.152), channel_id=1, source_target_pairs={{0,8},{8,16},{16,24},{24,32},{32,40},{40,48},{48,56},{56,64},{64,7... | collective-permute-start | bytes 6152 | tf_op jit(solution)/shard_map/ppermute | solution.py:16
  57.9 5.1 %copy-start = (f32[2048,256]{1,0:T(8,128)}, f32[2048,256]{1,0:T(8,128)S(1)}, u32[]{:S(2)}) copy-start(f32[2048,256]{1,0:T(8,128)S(1)} %fusion.42) | copy-start | bytes 6291460
  77.4 2.9 copy-start.1
  80.3 6.8 %copy-start.5 = (f32[1,1,512]{2,1,0:T(1,128)S(1)}, f32[1,1,512]{2,1,0:T(1,128)}, u32[]{:S(2)}) copy-start(f32[1,1,512]{2,1,0:T(1,128)} %param.19) | copy-start | bytes 6148
  82.5 63.6 %collective-permute-start = (f32[2048,256]{1,0:T(8,128)}, f32[2048,256]{1,0:T(8,128)}, u32[]{:S(2)}, u32[]{:S(2)}) collective-permute-start(f32[2048,256]{1,0:T(8,128)} %convolution_subtract_fusion.3), channel_id=1, source_target_pairs={{0,8},{8,16},{16,24},{24,32},{32,40},{40,48},{48,56},{56,64},{64,7... | collective-permute-start | bytes 6291464 | tf_op jit(solution)/shard_map/ppermute | solution.py:16
  87.8 44.4 %collective-permute-start.4 = (f32[2048,1]{0,1:T(1,128)S(1)}, f32[2048,1]{0,1:T(1,128)S(1)}, u32[]{:S(2)}, u32[]{:S(2)}) collective-permute-start(f32[2048,1]{0,1:T(1,128)S(1)} %fusion.11), channel_id=1, source_target_pairs={{0,8},{8,16},{16,24},{24,32},{32,40},{40,48},{48,56},{56,64},{64,7... | collective-permute-start | bytes 24584 | tf_op jit(solution)/shard_map/ppermute | solution.py:16
  136.2 9.8 %collective-permute-start.5 = (f32[2048,1]{0,1:T(1,128)S(1)}, f32[2048,1]{0,1:T(1,128)S(1)}, u32[]{:S(2)}, u32[]{:S(2)}) collective-permute-start(f32[2048,1]{0,1:T(1,128)S(1)} %fusion.10), channel_id=1, source_target_pairs={{0,16},{8,24},{16,32},{24,40},{32,48},{40,56},{48,64},{56,72},{64,... | collective-permute-start | bytes 24584 | tf_op jit(solution)/shard_map/ppermute | solution.py:16
  141.7 94.5 %collective-permute-start.2 = (bf16[1,2048,512]{2,1,0:T(8,128)(2,1)S(1)}, bf16[1,2048,512]{2,1,0:T(8,128)(2,1)}, u32[]{:S(2)}, u32[]{:S(2)}) collective-permute-start(bf16[1,2048,512]{2,1,0:T(8,128)(2,1)S(1)} %copy.10), channel_id=1, source_target_pairs={{0,8},{8,16},{16,24},{24,32},{32,40},{40,48},{48,56},{56,64},{64,7... | collective-permute-start | bytes 6291464 | tf_op jit(solution)/shard_map/ppermute | solution.py:16
  159.6 123.2 %collective-permute-start.1 = (f32[2048,256]{1,0:T(8,128)}, f32[2048,256]{1,0:T(8,128)}, u32[]{:S(2)}, u32[]{:S(2)}) collective-permute-start(f32[2048,256]{1,0:T(8,128)} %fusion.1), channel_id=1, source_target_pairs={{0,16},{8,24},{16,32},{24,40},{32,48},{40,56},{48,64},{56,72},{64,... | collective-permute-start | bytes 6291464 | tf_op jit(solution)/shard_map/ppermute | solution.py:16
